TPU v7x, 512 devices: a whole 4x4x16 slice. The times are simulated.
512 devices in a mesh: dp: 64 (over y, z), mp: 8 (over x, core).
Axes of the slice: x: 4, y: 4, z: 16, core: 2. Of those that a mesh axis runs over, the one named last changes fastest.
Arguments:
- x_in: bfloat16 [25600, 2048], P('dp'), may hold values from -6 to 6
- cotangent: bfloat16 [25600, 7168], P('dp', 'mp'), may hold values from -6 to 6
- w_gate: bfloat16 [2048, 7168], P('dp', 'mp'), may hold values from -0.125 to 0.125
- w_up: bfloat16 [2048, 7168], P('dp', 'mp'), may hold values from -0.125 to 0.125
- send_counts: int32 [64, 64], P('dp'), may hold values from 0 to 4, as said below
- recv_counts: int32 [64, 64], P('dp'), may hold values from 0 to 4, as said below
Outputs:
- grad_x: bfloat16 [25600, 2048], P('dp', 'mp')
- grad_gate: float32 [2048, 7168], P('dp', 'mp')
Inputs may be any that keep to these rules, and one draw needn't show every extreme that they name: `send_counts`: each entry is 0 to 4. A quarter of the indices only send and the rest only receive; one sending index sends 4 rows to every receiver, so its live rows reach 400. recv_counts is the transpose of send_counts.
All inputs are finite; a program needn't handle non-finite values.
Results may differ from a plain program's by a relative error of at most 0.014.
Values may be sent and summed in bfloat16 or wider, within the bound.
A program may use at most 64 MiB of HBM per device.

v0:
```python
import jax
import jax.numpy as jnp
from jax import lax
from jax.sharding import PartitionSpec as P

BAL = 208


def contract_last(left, right):
    return lax.dot_general(
        left, right, (((1,), (1,)), ((), ())), preferred_element_type=jnp.float32
    )


def swiglu_back(x_rows, cot_rows, gate_full, up_full, live_mask):
    gate_val = jnp.dot(x_rows, gate_full, preferred_element_type=jnp.float32)
    up_val = jnp.dot(x_rows, up_full, preferred_element_type=jnp.float32)
    sig = jax.nn.sigmoid(gate_val)
    cot_val = cot_rows.astype(jnp.float32)
    d_gate = jnp.where(
        live_mask[:, None], cot_val * up_val * sig * (1.0 + gate_val * (1.0 - sig)), 0.0
    ).astype(jnp.bfloat16)
    d_up = jnp.where(live_mask[:, None], cot_val * gate_val * sig, 0.0).astype(jnp.bfloat16)
    partial_value = contract_last(d_gate, gate_full) + contract_last(d_up, up_full)
    return (partial_value, d_gate)


def group_sum(partial_value):
    return lax.psum_scatter(
        partial_value.astype(jnp.bfloat16), "mp", scatter_dimension=1, tiled=True
    )


def on_device(x_in, cotangent, w_gate, w_up, send_counts, recv_counts):
    rows_cap = x_in.shape[0]
    width = x_in.shape[1]
    dev_count = lax.axis_size("dp")
    gate_full, up_full = (
        lax.all_gather(w_gate, "dp", axis=0, tiled=True),
        lax.all_gather(w_up, "dp", axis=0, tiled=True),
    )
    sent = send_counts[0]
    got = recv_counts[0]
    live_rows = BAL + jnp.sum(sent) - jnp.sum(got)
    live_mask = jnp.arange(rows_cap) < live_rows
    partial_value, d_gate = swiglu_back(x_in, cotangent, gate_full, up_full, live_mask)
    grad_x = group_sum(partial_value)
    block_rows = width // dev_count
    whole = lax.dot_general(
        x_in, d_gate, (((0,), (0,)), ((), ())), preferred_element_type=jnp.float32
    )
    pieces = lax.all_to_all(
        whole.reshape(dev_count, block_rows, whole.shape[1]),
        "dp",
        split_axis=0,
        concat_axis=0,
        tiled=True,
    )
    grad_gate = jnp.sum(pieces, axis=0)
    return (grad_x, grad_gate)


def solution(mesh):
    return jax.shard_map(
        on_device,
        mesh=mesh,
        in_specs=(
            P("dp", None),
            P("dp", "mp"),
            P("dp", "mp"),
            P("dp", "mp"),
            P("dp", None),
            P("dp", None),
        ),
        out_specs=(P("dp", "mp"), P("dp", "mp")),
        check_vma=False,
    )
```

profile of v0, /device:TPU:40, one launch (start us, length us, event | category | flops | bytes accessed | tf_op | source)
XLA Modules:
  0.0 655.1 jit_solution(2757115259836697737)
XLA Ops:
  7.2 0.0 copy-start
  7.2 0.0 all-gather.5.cloned.1.call-start
  7.2 0.7 all-gather.5.cloned.1.call-update
  7.9 0.0 all-gather.3.cloned.1.call-start
  8.0 0.7 all-gather.3.cloned.1.call-update
  8.7 1.3 reduce_sum.28
  10.0 1.3 reduce_sum.27
  12.6 0.0 copy-start.2
  12.6 146.4 %all-gather.5.cloned.1.call-done = bf16[2048,896]{1,0:T(8,128)(2,1)} async-done(((bf16[32,896]{1,0:T(8,128)(2,1)}), bf16[2048,896]{1,0:T(8,128)(2,1)}) %all-gather.5.cloned.1.call-update) | async-done | bytes 3670032 | tf_op jit(solution)/shard_map/all_gather | solution.py:39
  159.0 0.0 copy-done
  159.0 5.0 fusion.11
  164.0 137.7 %all-gather.3.cloned.1.call-done = bf16[2048,896]{1,0:T(8,128)(2,1)} async-done(((bf16[32,896]{1,0:T(8,128)(2,1)}), bf16[2048,896]{1,0:T(8,128)(2,1)}) %all-gather.3.cloned.1.call-update) | async-done | bytes 3670032 | tf_op jit(solution)/shard_map/all_gather | solution.py:40
  301.7 0.0 copy-done.2
  301.7 4.6 select_convert_fusion
  306.2 5.1 convolution_bitcast_fusion
  311.4 8.6 %copy.8 = f32[2048,896]{1,0:T(8,128)} copy(f32[2048,896]{0,1:T(8,128)} %convolution_bitcast_fusion) | data formatting | bytes 14680064 | tf_op jit(solution)/shard_map/dot_general | solution.py:49
  320.0 10.2 %all-to-all-start = ((f32[64,32,896]{2,1,0:T(8,128)}), f32[64,32,896]{2,1,0:T(8,128)}, u32[]{:S(2)}, u32[]{:S(2)}) async-start(f32[64,32,896]{2,1,0:T(8,128)} %bitcast.12), calls=%async_computation.1 | async-start | bytes 14680064 | tf_op jit(solution)/shard_map/all_to_all | solution.py:52
  330.2 0.0 reduce-scatter.2.cloned.1.call-start
  330.2 0.0 copy-start.1
  330.2 0.0 copy-start.3
  330.3 4.1 fusion.12
  334.3 0.0 copy-done.1
  334.3 0.0 copy-done.3
  334.4 3.1 add_convert_fusion
  337.5 0.0 reduce-scatter.2.cloned.1.call-update
  337.5 307.0 %all-to-all-done = f32[64,32,896]{2,1,0:T(8,128)} async-done(((f32[64,32,896]{2,1,0:T(8,128)}), f32[64,32,896]{2,1,0:T(8,128)}, u32[]{:S(2)}, u32[]{:S(2)}) %all-to-all-start) | async-done | bytes 7340064 | tf_op jit(solution)/shard_map/all_to_all | solution.py:52
  644.5 4.1 reduce_sum.29
  648.6 0.0 reduce-scatter.2.cloned.1.call-done
  (1 shorter events, 0.0 us)
Async XLA Ops:
  7.2 151.8 %copy-start = (bf16[400,2048]{1,0:T(8,128)(2,1)S(1)}, bf16[400,2048]{1,0:T(8,128)(2,1)}, u32[]{:S(2)}) copy-start(bf16[400,2048]{1,0:T(8,128)(2,1)} %param.6) | copy-start | bytes 4915204
  7.2 151.8 %all-gather.5.cloned.1.call-start = ((), (), s32[]{:S(2)}) async-start(), calls=%async_computation.3 | async-start | bytes 3727360 | tf_op jit(solution)/shard_map/all_gather | solution.py:39
  7.9 293.8 %all-gather.3.cloned.1.call-start = ((), (), s32[]{:S(2)}) async-start(), calls=%async_computation.2 | async-start | bytes 3727360 | tf_op jit(solution)/shard_map/all_gather | solution.py:40
  12.6 289.1 %copy-start.2 = (bf16[400,896]{1,0:T(8,128)(2,1)S(1)}, bf16[400,896]{1,0:T(8,128)(2,1)}, u32[]{:S(2)}) copy-start(bf16[400,896]{1,0:T(8,128)(2,1)} %param.7) | copy-start | bytes 2150404
  320.0 324.5 %all-to-all-start = ((f32[64,32,896]{2,1,0:T(8,128)}), f32[64,32,896]{2,1,0:T(8,128)}, u32[]{:S(2)}, u32[]{:S(2)}) async-start(f32[64,32,896]{2,1,0:T(8,128)} %bitcast.12), calls=%async_computation.1 | async-start | bytes 14680064 | tf_op jit(solution)/shard_map/all_to_all | solution.py:52
  330.2 318.4 %reduce-scatter.2.cloned.1.call-start = ((), (), s32[]{:S(2)}) async-start(), calls=%async_computation.4 | async-start | bytes 1843200 | tf_op jit(solution)/shard_map/reduce_scatter | solution.py:29
  330.2 4.1 copy-start.1
  330.2 4.1 copy-start.3
Sparse Core Ops, SparseCore 0:
  11.0 147.9 all-gather.4
  161.9 139.7 all-gather.2
  337.6 42.0 reduce-scatter.1
where the time goes:
time: 656 us; the launch traced here: 655 us
  waiting for transfers between devices  592 us (90%)
  matrix products  21.9 us (3%)
  between operations  15.1 us (2%)
  starting transfers between devices  10.3 us (2%)
  local copies, waits for them, and re-layouts  8.61 us (1%)
  other arithmetic  6.68 us (1%)
    all_to_all x1, waiting for transfers between devices, on_device(): lax.all_to_all(whole.reshape(dev_count, block_rows, whole.shape[1]), 'dp'...  307 us
    all_gather x1, waiting for transfers between devices, on_device(): lax.all_gather(w_gate, 'dp', axis=0, tiled=True)  146 us
    all_gather x1, waiting for transfers between devices, on_device(): lax.all_gather(w_up, 'dp', axis=0, tiled=True)  138 us
  transfers between devices with their start and end apart: 4, of which 3 were waited for; matrix products, arithmetic and copies ran while one was open for 3% of the time, Pallas kernels for 0%

commit v1 on v0

--- a/solution.py
+++ b/solution.py
@@ -4,6 +4,11 @@
 from jax.sharding import PartitionSpec as P
 
 BAL = 208
+
+
+def all_by_exchange(x, mesh_axis, dim):
+    stack = jnp.stack([x] * lax.axis_size(mesh_axis))
+    return jnp.concatenate(lax.all_to_all(stack, mesh_axis, 0, 0), axis=dim)
 
 
 def contract_last(left, right):
@@ -37,7 +42,7 @@
     dev_count = lax.axis_size("dp")
     gate_full, up_full = (
         lax.all_gather(w_gate, "dp", axis=0, tiled=True),
-        lax.all_gather(w_up, "dp", axis=0, tiled=True),
+        all_by_exchange(w_up, "dp", 0),
     )
     sent = send_counts[0]
     got = recv_counts[0]

time: 656 us -> 595 us (0.907)
  the two profiles are of different devices: /device:TPU:40 before, /device:TPU:6 now
where the time goes in v1:
time: 595 us; the launch traced here: 594 us
  waiting for transfers between devices  508 us (85%)
  starting transfers between devices  29.6 us (5%)
  matrix products  24 us (4%)
  between operations  15.4 us (3%)
  local copies, waits for them, and re-layouts  11.6 us (2%)
    all_to_all x1, waiting for transfers between devices, on_device(): lax.all_to_all(whole.reshape(dev_count, block_rows, whole.shape[1]), 'dp'...  310 us
    all_gather x1, waiting for transfers between devices, on_device(): lax.all_gather(w_gate, 'dp', axis=0, tiled=True)  198 us
    all_to_all x1, starting transfers between devices, all_by_exchange(): return jnp.concatenate(lax.all_to_all(stack, mesh_axis, 0, 0), axis=dim)  19.1 us
  transfers between devices with their start and end apart: 4, of which 2 were waited for; matrix products, arithmetic and copies ran while one was open for 3% of the time, Pallas kernels for 0%

profile of v1, /device:TPU:6, one launch (start us, length us, event | category | flops | bytes accessed | tf_op | source)
XLA Modules:
  0.0 594.1 jit_solution(46315861394344706)
XLA Ops:
  7.2 0.0 copy-start
  7.2 3.0 stack.2
  10.2 0.0 copy-start.2
  10.2 0.0 copy-start.3
  10.2 19.1 %all-to-all-start = ((bf16[64,32,896]{2,1,0:T(8,128)(2,1)}), bf16[64,32,896]{2,1,0:T(8,128)(2,1)}, u32[]{:S(2)}, u32[]{:S(2)}) async-start(bf16[64,32,896]{2,1,0:T(8,128)(2,1)} %stack.2), calls=%async_computation | async-start | bytes 7340032 | tf_op jit(solution)/shard_map/all_to_all | solution.py:11
  29.3 0.0 all-gather.2.cloned.1.call-start
  29.3 0.7 all-gather.2.cloned.1.call-update
  30.0 0.0 copy-done.2
  30.0 0.6 reduce_sum.28
  30.7 0.0 copy-done.3
  30.7 0.6 reduce_sum.27
  32.6 0.0 copy-start.1
  32.6 197.9 %all-gather.2.cloned.1.call-done = bf16[2048,896]{1,0:T(8,128)(2,1)} async-done(((bf16[32,896]{1,0:T(8,128)(2,1)}), bf16[2048,896]{1,0:T(8,128)(2,1)}) %all-gather.2.cloned.1.call-update) | async-done | bytes 3670032 | tf_op jit(solution)/shard_map/all_gather | solution.py:44
  230.5 0.0 copy-done
  230.5 5.0 fusion.11
  235.5 0.0 all-to-all-done
  235.5 0.0 copy-done.1
  235.5 4.6 select_convert_fusion
  240.1 5.1 convolution_bitcast_fusion
  245.2 8.6 %copy.8 = f32[2048,896]{1,0:T(8,128)} copy(f32[2048,896]{0,1:T(8,128)} %convolution_bitcast_fusion) | data formatting | bytes 14680064 | tf_op jit(solution)/shard_map/dot_general | solution.py:54
  253.8 10.4 %all-to-all-start.1 = ((f32[64,32,896]{2,1,0:T(8,128)}), f32[64,32,896]{2,1,0:T(8,128)}, u32[]{:S(2)}, u32[]{:S(2)}) async-start(f32[64,32,896]{2,1,0:T(8,128)} %bitcast.13), calls=%async_computation.2 | async-start | bytes 14680064 | tf_op jit(solution)/shard_map/all_to_all | solution.py:57
  264.2 0.0 reduce-scatter.2.cloned.1.call-start
  264.3 0.0 copy-start.4
  264.3 4.0 fusion.12
  268.3 0.0 copy-done.4
  268.3 5.2 add_convert_fusion
  273.5 0.0 reduce-scatter.2.cloned.1.call-update
  273.6 309.6 %all-to-all-done.1 = f32[64,32,896]{2,1,0:T(8,128)} async-done(((f32[64,32,896]{2,1,0:T(8,128)}), f32[64,32,896]{2,1,0:T(8,128)}, u32[]{:S(2)}, u32[]{:S(2)}) %all-to-all-start.1) | async-done | bytes 7340064 | tf_op jit(solution)/shard_map/all_to_all | solution.py:57
  583.1 4.1 reduce_sum.29
  587.2 0.0 reduce-scatter.2.cloned.1.call-done
  (1 shorter events, 0.0 us)
Async XLA Ops:
  7.2 223.3 %copy-start = (bf16[400,2048]{1,0:T(8,128)(2,1)S(1)}, bf16[400,2048]{1,0:T(8,128)(2,1)}, u32[]{:S(2)}) copy-start(bf16[400,2048]{1,0:T(8,128)(2,1)} %param.6) | copy-start | bytes 4915204
  10.2 19.8 %copy-start.2 = (s32[1,64]{1,0:T(1,128)S(1)}, s32[1,64]{1,0:T(1,128)}, u32[]{:S(2)}) copy-start(s32[1,64]{1,0:T(1,128)} %param.11) | copy-start | bytes 772
  10.2 20.5 %copy-start.3 = (s32[1,64]{1,0:T(1,128)S(1)}, s32[1,64]{1,0:T(1,128)}, u32[]{:S(2)}) copy-start(s32[1,64]{1,0:T(1,128)} %param.10) | copy-start | bytes 772
  10.2 225.3 %all-to-all-start = ((bf16[64,32,896]{2,1,0:T(8,128)(2,1)}), bf16[64,32,896]{2,1,0:T(8,128)(2,1)}, u32[]{:S(2)}, u32[]{:S(2)}) async-start(bf16[64,32,896]{2,1,0:T(8,128)(2,1)} %stack.2), calls=%async_computation | async-start | bytes 7340032 | tf_op jit(solution)/shard_map/all_to_all | solution.py:11
  29.3 201.2 %all-gather.2.cloned.1.call-start = ((), (), s32[]{:S(2)}) async-start(), calls=%async_computation.3 | async-start | bytes 3727360 | tf_op jit(solution)/shard_map/all_gather | solution.py:44
  32.6 202.9 %copy-start.1 = (bf16[400,896]{1,0:T(8,128)(2,1)S(1)}, bf16[400,896]{1,0:T(8,128)(2,1)}, u32[]{:S(2)}) copy-start(bf16[400,896]{1,0:T(8,128)(2,1)} %param.7) | copy-start | bytes 2150404
  253.8 329.3 %all-to-all-start.1 = ((f32[64,32,896]{2,1,0:T(8,128)}), f32[64,32,896]{2,1,0:T(8,128)}, u32[]{:S(2)}, u32[]{:S(2)}) async-start(f32[64,32,896]{2,1,0:T(8,128)} %bitcast.13), calls=%async_computation.2 | async-start | bytes 14680064 | tf_op jit(solution)/shard_map/all_to_all | solution.py:57
  264.2 323.0 %reduce-scatter.2.cloned.1.call-start = ((), (), s32[]{:S(2)}) async-start(), calls=%async_computation.4 | async-start | bytes 1843200 | tf_op jit(solution)/shard_map/reduce_scatter | solution.py:34
  264.3 4.0 copy-start.4
Sparse Core Ops, SparseCore 0:
  33.1 197.3 all-gather.1
  273.7 38.5 reduce-scatter.1
